TPU v7x, 32 devices: a whole 2x2x4 slice. The times are simulated.
32 devices in a mesh: gx: 8 (over y, x, core), gy: 4 (over z).
Axes of the slice: x: 2, y: 2, z: 4, core: 2. Of those that a mesh axis runs over, the one named last changes fastest.
Arguments:
- fine_nodes: bfloat16 [32, 8, 128, 512], P('gx', 'gy'), may hold values from -6 to 6
- edge_states: bfloat16 [8, 4, 64, 128, 512], P('gx', 'gy'), may hold values from -6 to 6
- middle_nodes: bfloat16 [8, 4, 128, 512], P('gx', 'gy'), may hold values from -6 to 6
- coarse_nodes: bfloat16 [256, 512], P(('gx', 'gy')), may hold values from -6 to 6
- edge_sources: int32 [8, 4, 64, 128], P('gx', 'gy'), may hold values from 0 to 3071, as said below
- target_blocks: int32 [8, 4, 64], P('gx', 'gy'), may hold values from 0 to 7
- target_nodes: int32 [8, 4, 64, 128], P('gx', 'gy'), may hold values from 0 to 127
- live_blocks: int32 [8, 4], P('gx', 'gy'), may hold values from 32 to 64, as said below
- fine_parent: int32 [32, 8, 128], P('gx', 'gy'), may hold values from 0 to 127
- fine_weight: float32 [32, 8, 128], P('gx', 'gy'), may hold values from 0.2 to 0.6
- middle_parent: int32 [8, 4, 128], P('gx', 'gy'), may hold values from 0 to 255, as said below
- middle_weight: float32 [8, 4, 128], P('gx', 'gy'), may hold values from 0.1 to 0.3
- edge_in: bfloat16 [3, 512, 512], replicated, may hold values from -0.15625 to 0.15625
- edge_bias: float32 [512], replicated, may hold values from -3 to 3
- edge_out: bfloat16 [512, 512], replicated, may hold values from -0.25 to 0.25
- edge_bias_two: float32 [512], replicated, may hold values from -3 to 3
- edge_gain: float32 [512], replicated, may hold values from 0.1 to 1.9
- node_in: bfloat16 [2, 512, 512], replicated, may hold values from -0.1875 to 0.1875
- node_bias: float32 [512], replicated, may hold values from -3 to 3
- node_out: bfloat16 [512, 512], replicated, may hold values from -0.25 to 0.25
- node_bias_two: float32 [512], replicated, may hold values from -3 to 3
- node_gain: float32 [512], replicated, may hold values from 0.1 to 1.9
- coarse_in: bfloat16 [2, 512, 512], replicated, may hold values from -0.1875 to 0.1875
- coarse_bias: float32 [512], replicated, may hold values from -3 to 3
- coarse_out: bfloat16 [512, 512], replicated, may hold values from -0.25 to 0.25
- coarse_bias_two: float32 [512], replicated, may hold values from -3 to 3
- coarse_gain: float32 [512], replicated, may hold values from 0.1 to 1.9
Outputs:
- fine_result: bfloat16 [32, 8, 128, 512], P('gx', 'gy')
- edge_result: bfloat16 [8, 4, 64, 128, 512], P('gx', 'gy')
- middle_result: bfloat16 [8, 4, 128, 512], P('gx', 'gy')
- coarse_result: bfloat16 [256, 512], P(('gx', 'gy'))
Inputs may be any that keep to these rules, and one draw needn't show every extreme that they name: `edge_sources`: sources lie in the device's own blocks or in the blocks touching them (diagonals too), never outside the grid. `live_blocks`: some device has all 64 slots live in every draw. `middle_parent`: coarse node c is owned by device c // 8 in the order of gx+gy. Of the 128 middle nodes of one device, exactly 4 have their parent among the coarse nodes of each owner.
All inputs are finite; a program needn't handle non-finite values.
Results may differ from a plain program's by a relative error of at most 0.0075.
Values may be sent and summed in bfloat16 or wider, within the bound.
A program may use at most 192 MiB of HBM per device.

v0:
```python
import functools

import jax
import jax.numpy as jnp
from jax import lax
from jax.experimental import pallas as pl
from jax.experimental.pallas import tpu as pltpu
from jax.sharding import PartitionSpec as P

epsilon = 1e-05
f32 = jnp.float32
bf16 = jnp.bfloat16
PAIR = 4


def layer_norm(values, gain_vec):
    centred = values - jnp.mean(values, axis=-1, keepdims=True)
    spread = jnp.mean(centred * centred, axis=-1, keepdims=True)
    return centred * lax.rsqrt(spread + epsilon) * gain_vec


def first_dims(left, right):
    return lax.dot_general(left, right, (((0,), (0,)), ((), ())), preferred_element_type=f32)


def split_two(values):
    high = values.astype(bf16)
    return high, (values - high.astype(f32)).astype(bf16)


def exchange_kernel(
    grid_shape,
    own_ref,
    mid_ref,
    parent_ref,
    weight_ref,
    mid_parent_ref,
    mid_weight_ref,
    coarse_ref,
    win_ref,
    bias_ref,
    wout_ref,
    bias_two_ref,
    gain_ref,
    window_ref,
    everyone_ref,
    result_ref,
    middle_ref,
    partial,
    arrived_x,
    summed_x,
    arrived_y,
    side_send,
    side_recv,
    edge_send,
    edge_recv,
    corner_send,
    corner_recv,
    sx_send,
    sx_recv,
    sy_send,
    sy_recv,
    gx_send,
    gx_recv,
    gy_send,
    gy_recv,
):
    count_x, count_y = grid_shape
    rows_x, rows_y, blk, width = own_ref.shape
    mids = mid_ref.shape[0]
    at_x, at_y = lax.axis_index("gx"), lax.axis_index("gy")
    peers_x = [lax.rem(at_x + offset, count_x) for offset in range(1, count_x)]
    peers_y = [lax.rem(at_y + offset, count_y) for offset in range(1, count_y)]
    mesh_ids = pl.DeviceIdType.MESH

    barrier = pltpu.get_barrier_semaphore()
    for x in peers_x:
        pl.semaphore_signal(barrier, inc=1, device_id=(x, at_y), device_id_type=mesh_ids)
    for y in peers_y:
        pl.semaphore_signal(barrier, inc=1, device_id=(at_x, y), device_id_type=mesh_ids)
    pl.semaphore_wait(barrier, count_x + count_y - 2)

    def remote(src, dst, send, recv, x, y):
        return pltpu.make_async_remote_copy(
            src_ref=src,
            dst_ref=dst,
            send_sem=send,
            recv_sem=recv,
            device_id=(x, y),
            device_id_type=mesh_ids,
        )

    def has_x(x):
        return (x >= 0) & (x < count_x)

    def has_y(y):
        return (y >= 0) & (y < count_y)

    pieces = [(0, 1), (rows_x - 1, 1)] + ([(1, rows_x - 2)] if rows_x > 2 else [])
    ways = [1, -1]

    def side_copy(way, piece, y):
        first, length = pieces[piece]
        column = rows_y - 1 if ways[way] == 1 else 0
        to = 0 if ways[way] == 1 else rows_y + 1
        return remote(
            own_ref.at[pl.ds(first, length), pl.ds(column, 1)],
            window_ref.at[pl.ds(first + 1, length), pl.ds(to, 1)],
            side_send.at[way, piece],
            side_recv.at[way, piece],
            at_x,
            y,
        )

    def edge_copy(way, x):
        row = rows_x - 1 if ways[way] == 1 else 0
        to = 0 if ways[way] == 1 else rows_x + 1
        return remote(
            own_ref.at[row], window_ref.at[to, pl.ds(1, rows_y)], edge_send.at[way], edge_recv.at[way], x, at_y
        )

    def corner_copy(way, side, x):
        row = rows_x if ways[way] == 1 else 1
        to = 0 if ways[way] == 1 else rows_x + 1
        column = 0 if ways[side] == 1 else rows_y + 1
        return remote(
            window_ref.at[row, column],
            window_ref.at[to, column],
            corner_send.at[way, side],
            corner_recv.at[way, side],
            x,
            at_y,
        )

    def start_sides(piece):
        for way in range(2):

            @pl.when(has_y(at_y + ways[way]))
            def _():
                side_copy(way, piece, at_y + ways[way]).start()

    def sum_x_copy(slot_from, slot_to, x):
        return remote(
            partial.at[slot_from], arrived_x.at[slot_to], sx_send.at[slot_from], sx_recv.at[slot_to], x, at_y
        )

    def sum_y_copy(slot_from, slot_to, y):
        return remote(
            summed_x.at[slot_from], arrived_y.at[slot_to], sy_send.at[slot_from], sy_recv.at[slot_to], at_x, y
        )

    def full_y_copy(slot, y):
        here = everyone_ref.at[at_x, slot]
        return remote(here, here, gy_send.at[y], gy_recv.at[slot], at_x, y)

    def full_x_copy(slot, x):
        here = everyone_ref.at[slot]
        return remote(here, here, gx_send.at[x], gx_recv.at[slot], x, at_y)

    start_sides(0)
    start_sides(1)

    own = own_ref[...].reshape(rows_x * rows_y * blk, width)
    ids = lax.broadcasted_iota(jnp.int32, (mids, own.shape[0]), 0)
    high, low = split_two(jnp.where(ids == parent_ref[...], weight_ref[...], 0.0))
    middle = mid_ref[...].astype(f32) + jnp.dot(high, own, preferred_element_type=f32)
    middle = (middle + jnp.dot(low, own, preferred_element_type=f32)).astype(bf16)
    ids = lax.broadcasted_iota(jnp.int32, (count_x * count_y * coarse_ref.shape[0], mids), 0)
    high, low = split_two(jnp.where(ids == mid_parent_ref[...], mid_weight_ref[...], 0.0))
    sums = jnp.dot(high, middle, preferred_element_type=f32)
    sums = sums + jnp.dot(low, middle, preferred_element_type=f32)
    partial[...] = sums.reshape(partial.shape)
    middle_ref[...] = middle

    for x in peers_x:
        sum_x_copy(x, at_x, x).start()
    for way in range(2):

        @pl.when(has_x(at_x + ways[way]))
        def _():
            edge_copy(way, at_x + ways[way]).start()

    total = partial[at_x]
    for x in peers_x:
        sum_x_copy(x, x, x).wait_recv()
        total = total + arrived_x[x]
    summed_x[...] = total

    for side in range(2):
        from_y = at_y - ways[side]

        @pl.when(has_y(from_y))
        def _():
            side_copy(side, 0, from_y).wait_recv()
            side_copy(side, 1, from_y).wait_recv()
            for way in range(2):

                @pl.when(has_x(at_x + ways[way]))
                def _():
                    corner_copy(way, side, at_x + ways[way]).start()

    for y in peers_y:
        sum_y_copy(y, at_y, y).start()
    if len(pieces) > 2:
        start_sides(2)
    restricted = summed_x[at_y]
    for y in peers_y:
        sum_y_copy(y, y, y).wait_recv()
        restricted = restricted + arrived_y[y]

    coarse = coarse_ref[...]
    pre = jnp.dot(coarse, win_ref[0], preferred_element_type=f32)
    pre = pre + jnp.dot(restricted.astype(bf16), win_ref[1], preferred_element_type=f32)
    pre = (pre + bias_ref[...]) * 0.5
    hidden = (pre + pre * jnp.tanh(pre)).astype(bf16)
    output = jnp.dot(hidden, wout_ref[...], preferred_element_type=f32) + bias_two_ref[...]
    result = (coarse.astype(f32) + layer_norm(output, gain_ref[...])).astype(bf16)
    everyone_ref[at_x, at_y] = result
    result_ref[...] = result

    for way in range(2):

        @pl.when(has_x(at_x - ways[way]))
        def _():
            edge_copy(way, at_x - ways[way]).wait_recv()

    for y in peers_y:
        full_y_copy(at_y, y).start()
    for y in peers_y:
        full_y_copy(y, y).wait_recv()
    for x in peers_x:
        full_x_copy(at_x, x).start()

    for way in range(2):

        @pl.when(has_x(at_x + ways[way]))
        def _():
            edge_copy(way, at_x + ways[way]).wait_send()

        @pl.when(has_y(at_y + ways[way]))
        def _():
            for piece in range(len(pieces)):
                side_copy(way, piece, at_y + ways[way]).wait_send()

        if len(pieces) > 2:

            @pl.when(has_y(at_y - ways[way]))
            def _():
                side_copy(way, 2, at_y - ways[way]).wait_recv()

        for side in range(2):

            @pl.when(has_y(at_y - ways[side]) & has_x(at_x + ways[way]))
            def _():
                corner_copy(way, side, at_x + ways[way]).wait_send()

            @pl.when(has_y(at_y - ways[side]) & has_x(at_x - ways[way]))
            def _():
                corner_copy(way, side, at_x - ways[way]).wait_recv()

    for x in peers_x:
        sum_x_copy(x, at_x, x).wait_send()
        full_x_copy(at_x, x).wait_send()
        full_x_copy(x, x).wait_recv()
    for y in peers_y:
        sum_y_copy(y, at_y, y).wait_send()
        full_y_copy(at_y, y).wait_send()


def exchange(own, middle, parents, weights, mid_parents, mid_weights, coarse, params):
    rows_x, rows_y, blk, width = own.shape
    count_x, count_y = lax.axis_size("gx"), lax.axis_size("gy")
    coarse_own = coarse.shape[0]
    coarse_in, bias, coarse_out, bias_two, gain = params
    row = lambda array: array.reshape(1, -1)
    vmem = pl.BlockSpec(memory_space=pltpu.VMEM)
    dma = pltpu.SemaphoreType.DMA
    return pl.pallas_call(
        functools.partial(exchange_kernel, (count_x, count_y)),
        in_specs=[vmem] * 12,
        out_specs=[vmem] * 4,
        out_shape=[
            jax.ShapeDtypeStruct((rows_x + 2, rows_y + 2, blk, width), bf16),
            jax.ShapeDtypeStruct((count_x, count_y, coarse_own, width), bf16),
            jax.ShapeDtypeStruct((coarse_own, width), bf16),
            jax.ShapeDtypeStruct(middle.shape, bf16),
        ],
        scratch_shapes=[
            pltpu.VMEM((count_x, count_y, coarse_own, width), f32),
            pltpu.VMEM((count_x, count_y, coarse_own, width), f32),
            pltpu.VMEM((count_y, coarse_own, width), f32),
            pltpu.VMEM((count_y, coarse_own, width), f32),
            dma((2, 3)),
            dma((2, 3)),
            dma((2,)),
            dma((2,)),
            dma((2, 2)),
            dma((2, 2)),
            dma((count_x,)),
            dma((count_x,)),
            dma((count_y,)),
            dma((count_y,)),
            dma((count_x,)),
            dma((count_x,)),
            dma((count_y,)),
            dma((count_y,)),
        ],
        compiler_params=pltpu.CompilerParams(collective_id=0, has_side_effects=True),
        name="exchange",
    )(
        own,
        middle,
        row(parents),
        row(weights),
        row(mid_parents),
        row(mid_weights),
        coarse,
        coarse_in,
        row(bias),
        coarse_out,
        row(bias_two),
        row(gain),
    )


def edge_kernel(
    shape,
    src_ref,
    tb_ref,
    live_ref,
    own_ref,
    window_ref,
    edge_ref,
    tgt_ref,
    win_ref,
    bias_ref,
    wout_ref,
    bias_two_ref,
    gain_ref,
    out_ref,
    agg_ref,
    table,
    target_table,
    first_w,
    buf_a,
    buf_b,
    total,
):
    rows_x, rows_y, blk, width = shape
    lanes = table.shape[-1]
    parts = width // lanes
    step = pl.program_id(0)
    steps = pl.num_programs(0)
    per_step = 2 * PAIR
    live = live_ref[0]

    def gather(first_block, buf):
        base = first_block * blk
        for e in range(PAIR * blk):
            row = src_ref[base + e] * parts
            at = (e // 8) * (8 * parts) + e % 8
            buf[pl.ds(at, parts, stride=8), :] = table[pl.ds(pl.multiple_of(row, parts), parts), :]

    def compute(first_block, local, buf):
        rows = PAIR * blk
        start = local * blk
        edges = edge_ref[pl.ds(start, rows), :]
        pre = jnp.dot(edges, first_w[...], preferred_element_type=f32)
        found = buf[...].reshape(rows // 8, parts, 8, lanes)
        found = jnp.concatenate(
            [found[:, c].reshape(rows, lanes) for c in range(parts)], axis=1
        )
        picks = []
        from_target = []
        for k in range(PAIR):
            target = tgt_ref[pl.ds(local + k, 1), :]
            pick = (lax.broadcasted_iota(jnp.int32, (blk, blk), 0) == target).astype(f32).astype(bf16)
            picks.append(pick)
            here = pl.multiple_of(tb_ref[first_block + k] * blk, blk)
            from_target.append(first_dims(pick, target_table[pl.ds(here, blk), :]))
        half = pre + jnp.concatenate(from_target, axis=0) + found
        hidden = (half + half * jnp.tanh(half)).astype(bf16)
        output = jnp.dot(hidden, wout_ref[...], preferred_element_type=f32) + bias_two_ref[...]
        centred = output - jnp.mean(output, axis=-1, keepdims=True)
        spread = jnp.mean(centred * centred, axis=-1, keepdims=True)
        normed = centred * lax.rsqrt(spread + epsilon)
        for k in range(PAIR):
            alive = (first_block + k < live).astype(f32)
            part = slice(k * blk, (k + 1) * blk)
            message = (normed[part] * (gain_ref[...] * alive)).astype(bf16)
            out_ref[pl.ds(start + k * blk, blk), :] = edges[part] + message
            here = pl.multiple_of(tb_ref[first_block + k] * blk, blk)
            total[pl.ds(here, blk), :] += jnp.dot(picks[k], message, preferred_element_type=f32)

    @pl.when(step == 0)
    def _():
        total[...] = jnp.zeros_like(total)
        first_w[...] = win_ref[0] * 0.5
        for a in range(rows_x + 2):
            for b in range(rows_y + 2):
                number = a * (rows_y + 2) + b
                mine = 1 <= a <= rows_x and 1 <= b <= rows_y
                rows = own_ref[a - 1, b - 1] if mine else window_ref[a, b]
                made = jnp.dot(rows, win_ref[1], preferred_element_type=f32)
                made = (made + bias_ref[...]) * 0.5
                for c in range(parts):
                    at = pl.ds(number * blk * parts + c, blk, stride=parts)
                    table[at, :] = made[:, c * lanes : (c + 1) * lanes]
                if mine:
                    made = jnp.dot(rows, win_ref[2], preferred_element_type=f32) * 0.5
                    at = ((a - 1) * rows_y + b - 1) * blk
                    target_table[pl.ds(at, blk), :] = made.astype(bf16)
        gather(0, buf_a)

    @pl.when(step * per_step < live)
    def _():
        first = step * per_step
        gather(first + PAIR, buf_b)
        compute(first, 0, buf_a)
        following = jnp.minimum(step + 1, steps - 1) * per_step
        gather(following, buf_a)
        compute(first + PAIR, PAIR, buf_b)

    @pl.when(step * per_step >= live)
    def _():
        out_ref[...] = edge_ref[...]

    @pl.when(step == steps - 1)
    def _():
        agg_ref[...] = total[...].astype(bf16)


def run_edges(own, window, edges, sources, block_target, node_target, live, params):
    pieces = [own, window]
    rows_x, rows_y, blk, width = own.shape
    edge_in, bias, edge_out, bias_two, gain = params
    edge_blocks = edges.shape[0]
    per_step = 2 * PAIR
    lanes = 128
    whole = lambda array: pl.BlockSpec(array.shape, lambda i, *_: (0,) * array.ndim)
    flat = edges.reshape(edge_blocks * blk, width)
    targets = node_target.reshape(edge_blocks // per_step, per_step, blk)
    small = [bias.reshape(1, width), edge_out, bias_two.reshape(1, width), gain.reshape(1, width)]
    own_count = rows_x * rows_y * blk
    row_spec = pl.BlockSpec((per_step * blk, width), lambda i, *_: (i, 0))
    return pl.pallas_call(
        functools.partial(edge_kernel, own.shape),
        grid_spec=pltpu.PrefetchScalarGridSpec(
            num_scalar_prefetch=3,
            grid=(edge_blocks // per_step,),
            in_specs=[whole(p) for p in pieces]
            + [row_spec, pl.BlockSpec((None, per_step, blk), lambda i, *_: (i, 0, 0)), whole(edge_in)]
            + [whole(s) for s in small],
            out_specs=[row_spec, pl.BlockSpec((own_count, width), lambda i, *_: (0, 0))],
            scratch_shapes=[
                pltpu.VMEM(((rows_x + 2) * (rows_y + 2) * blk * (width // lanes), lanes), f32),
                pltpu.VMEM((own_count, width), bf16),
                pltpu.VMEM((width, width), bf16),
                pltpu.VMEM((PAIR * blk * width // lanes, lanes), f32),
                pltpu.VMEM((PAIR * blk * width // lanes, lanes), f32),
                pltpu.VMEM((own_count, width), f32),
            ],
        ),
        out_shape=[
            jax.ShapeDtypeStruct(flat.shape, bf16),
            jax.ShapeDtypeStruct((own_count, width), bf16),
        ],
        cost_estimate=pl.CostEstimate(
            flops=8 * flat.shape[0] * width * width,
            bytes_accessed=4 * flat.size,
            transcendentals=flat.size,
        ),
        name="edge_layer",
    )(sources.reshape(-1), block_target, live.reshape(1), *pieces, flat, targets, edge_in, *small)


def node_kernel(
    own_ref,
    agg_ref,
    parent_ref,
    weight_ref,
    mid_ref,
    mid_parent_ref,
    mid_weight_ref,
    coarse_ref,
    win_ref,
    bias_ref,
    wout_ref,
    bias_two_ref,
    gain_ref,
    out_ref,
    mid_out_ref,
    doubled,
):
    mids = mid_ref.shape[0]

    @pl.when(pl.program_id(0) == 0)
    def _():
        coarse = coarse_ref[...]
        ids = lax.broadcasted_iota(jnp.int32, (coarse.shape[0], mids), 0)
        spread = jnp.where(ids == mid_parent_ref[...], mid_weight_ref[...], 0.0)
        high, low = split_two(spread)
        value = mid_ref[...].astype(f32) + first_dims(high, coarse) + first_dims(low, coarse)
        value = value.astype(bf16)
        mid_out_ref[...] = value
        doubled[pl.ds(0, mids), :] = value
        doubled[pl.ds(mids, mids), :] = value

    own = own_ref[...]
    pre = jnp.dot(own, win_ref[0], preferred_element_type=f32)
    pre = (pre + jnp.dot(agg_ref[...], win_ref[1], preferred_element_type=f32) + bias_ref[...]) * 0.5
    hidden = (pre + pre * jnp.tanh(pre)).astype(bf16)
    output = jnp.dot(hidden, wout_ref[...], preferred_element_type=f32) + bias_two_ref[...]
    fine = own.astype(f32) + layer_norm(output, gain_ref[...])
    ids = lax.broadcasted_iota(jnp.int32, (mids, own.shape[0]), 0)
    high, low = split_two(jnp.where(ids == parent_ref[...], weight_ref[...], 0.0))
    from_middle = first_dims(jnp.concatenate([high, low], axis=0), doubled[...])
    out_ref[...] = (fine + from_middle).astype(bf16)


def run_nodes(own, agg, parents, weights, middle, mid_parents, mid_weights, coarse, params):
    count, width = own.shape
    node_in, bias, node_out, bias_two, gain = params
    tile = 256 if count % 256 == 0 else 128
    whole = lambda array: pl.BlockSpec(array.shape, lambda i: (0,) * array.ndim)
    rows = pl.BlockSpec((tile, width), lambda i: (i, 0))
    across = pl.BlockSpec((1, tile), lambda i: (0, i))
    row = lambda array: array.reshape(1, -1)
    fixed = [middle, row(mid_parents), row(mid_weights), coarse]
    fixed += [node_in, row(bias), node_out, row(bias_two), row(gain)]
    return pl.pallas_call(
        node_kernel,
        grid=(count // tile,),
        in_specs=[rows, rows, across, across] + [whole(f) for f in fixed],
        out_specs=[rows, whole(middle)],
        out_shape=[jax.ShapeDtypeStruct(own.shape, bf16), jax.ShapeDtypeStruct(middle.shape, bf16)],
        scratch_shapes=[pltpu.VMEM((2 * middle.shape[0], width), bf16)],
        cost_estimate=pl.CostEstimate(
            flops=8 * count * width * width, bytes_accessed=8 * own.size, transcendentals=own.size
        ),
        name="node_layer",
    )(own, agg, row(parents), row(weights), *fixed)


def body(
    fine_nodes,
    edge_states,
    middle_nodes,
    coarse_nodes,
    edge_sources,
    target_blocks,
    target_nodes,
    live_blocks,
    fine_parent,
    fine_weight,
    middle_parent,
    middle_weight,
    edge_in,
    edge_bias,
    edge_out,
    edge_bias_two,
    edge_gain,
    node_in,
    node_bias,
    node_out,
    node_bias_two,
    node_gain,
    coarse_in,
    coarse_bias,
    coarse_out,
    coarse_bias_two,
    coarse_gain,
):
    rows_x, rows_y, block_size, latent = fine_nodes.shape
    own_count = rows_x * rows_y * block_size
    own_rows = fine_nodes.reshape(own_count, latent)
    edge_params = (edge_in, edge_bias, edge_out, edge_bias_two, edge_gain)
    node_params = (node_in, node_bias, node_out, node_bias_two, node_gain)
    parents_local = fine_parent.reshape(own_count)
    weights_local = fine_weight.reshape(own_count)
    middle_rows = middle_nodes[0, 0]
    mid_parents = middle_parent[0, 0]
    mid_weights = middle_weight[0, 0]
    coarse_own = coarse_nodes.shape[0]
    devices = lax.axis_size(("gx", "gy"))
    window, everyone, coarse_result, middle_mid = exchange(
        fine_nodes,
        middle_rows,
        parents_local,
        weights_local,
        mid_parents,
        mid_weights,
        coarse_nodes,
        (coarse_in, coarse_bias, coarse_out, coarse_bias_two, coarse_gain),
    )
    everyone = everyone.reshape(devices * coarse_own, latent)
    edge_result, aggregate = run_edges(
        fine_nodes,
        window,
        edge_states[0, 0],
        edge_sources[0, 0],
        target_blocks[0, 0],
        target_nodes[0, 0],
        live_blocks[0, 0],
        edge_params,
    )
    fine_result, middle_result = run_nodes(
        own_rows,
        aggregate,
        parents_local,
        weights_local,
        middle_mid,
        mid_parents,
        mid_weights,
        everyone,
        node_params,
    )
    return (
        fine_result.reshape(fine_nodes.shape),
        edge_result.reshape(edge_states.shape),
        middle_result.reshape(middle_nodes.shape),
        coarse_result,
    )


def solution(mesh):
    placed = (
        P("gx", "gy", None, None),
        P("gx", "gy", None, None, None),
        P("gx", "gy", None, None),
        P(("gx", "gy"), None),
        P("gx", "gy", None, None),
        P("gx", "gy", None),
        P("gx", "gy", None, None),
        P("gx", "gy"),
        P("gx", "gy", None),
        P("gx", "gy", None),
        P("gx", "gy", None),
        P("gx", "gy", None),
        P(),
        P(),
        P(),
        P(),
        P(),
        P(),
        P(),
        P(),
        P(),
        P(),
        P(),
        P(),
        P(),
        P(),
        P(),
    )
    return jax.shard_map(
        body,
        mesh=mesh,
        in_specs=placed,
        out_specs=(
            P("gx", "gy", None, None),
            P("gx", "gy", None, None, None),
            P("gx", "gy", None, None),
            P(("gx", "gy"), None),
        ),
        check_vma=False,
    )
```

profile of v0, /device:TPU:1, one launch (start us, length us, event | category | flops | bytes accessed | tf_op | source)
XLA Modules:
  0.0 75.4 jit_solution(5637405338551605635)
XLA Ops:
  1.3 31.8 %exchange.1 = (bf16[6,4,128,512]{3,2,1,0:T(8,128)(2,1)}, bf16[8,4,8,512]{3,2,1,0:T(8,128)(2,1)}, bf16[8,512]{1,0:T(8,128)(2,1)}, bf16[128,512]{1,0:T(8,128)(2,1)}) custom-call(bf16[4,2,128,512]{3,2,1,0:T(8,128)(2,1)} %own_ref.3, bf16[128,512]{1,0:T(8,128)(2,1)} %bitcast.26, s32[1,1024]{1,0:T(1,128)} %bitcast.27, f32[1,1024]{1,0:T(1,128)} %bitcast.29, ...), custom_call_target="tpu_custom_call" | custom-call | tf_op jit(solution)/shard_map/exchange/pallas_call | solution.py:278
  33.1 0.0 copy-start
  33.1 34.9 %edge_layer.1 = (bf16[8192,512]{1,0:T(8,128)(2,1)}, bf16[1024,512]{1,0:T(8,128)(2,1)}) custom-call(s32[8192]{0:T(1024)} %bitcast.40, s32[64]{0:T(128)} %bitcast.48, s32[1]{0:T(128)} %bitcast.24.live_ref, bf16[4,2,128,512]{3,2,1,0:T(8,128)(2,1)} %own_ref.3, bf16[6,4,128,512]{3,2,1,0:T(8,128)(2,1)} %get-tuple-element.12.window_ref, ...), custom_call_target="tpu_custom_call" | custom-call | flops 17179869184 | bytes 16777216 | tf_op jit(solution)/shard_map/edge_layer/pallas_call | solution.py:446
  68.0 6.8 %node_layer.1 = (bf16[1024,512]{1,0:T(8,128)(2,1)}, bf16[128,512]{1,0:T(8,128)(2,1)}) custom-call(bf16[1024,512]{1,0:T(8,128)(2,1)} %bitcast.25, bf16[1024,512]{1,0:T(8,128)(2,1)} %get-tuple-element.13.agg_ref, s32[1,1024]{1,0:T(1,128)} %bitcast.28, f32[1,1024]{1,0:T(1,128)} %bitcast.30, bf16[128,512]{1,0:T(8,128)(2,1)} %get-tuple-element.14.mid_ref, ...), custom_call_target="tpu_custom_call" | custom-call | flops 2147483648 | bytes 4194304 | tf_op jit(solution)/shard_map/node_layer/pallas_call | solution.py:531
  74.8 0.0 copy-done
  74.8 0.6 copy.33
Async XLA Ops:
  33.1 41.7 %copy-start = (bf16[8,512]{1,0:T(8,128)(2,1)S(1)}, bf16[8,512]{1,0:T(8,128)(2,1)}, u32[]{:S(2)}) copy-start(bf16[8,512]{1,0:T(8,128)(2,1)} %get-tuple-element.27) | copy-start | bytes 24580
where the time goes:
time: 74.9 us; the launch traced here: 75.4 us
  Pallas kernels  73.5 us (98%)
  between operations  1.3 us (2%)
    pallas_call x1, Pallas kernels, run_edges(): pl.pallas_call(functools.partial(edge_kernel, own.shape), grid_spec=pltpu...  34.9 us
    pallas_call x1, Pallas kernels, exchange(): pl.pallas_call(functools.partial(exchange_kernel, (count_x, count_y)), in...  31.8 us
    pallas_call x1, Pallas kernels, run_nodes(): pl.pallas_call(node_kernel, grid=(count // tile,), in_specs=[rows, rows,...  6.83 us

commit v1 on v0

--- a/solution.py
+++ b/solution.py
@@ -11,6 +11,9 @@
 f32 = jnp.float32
 bf16 = jnp.bfloat16
 PAIR = 4
+FRONT_VMEM = 60 * 2**20
+EDGE_VMEM = 60 * 2**20
+TABLE = lambda *shape: jax.ShapeDtypeStruct(shape, f32)
 
 
 def layer_norm(values, gain_vec):
@@ -28,7 +31,7 @@
     return high, (values - high.astype(f32)).astype(bf16)
 
 
-def exchange_kernel(
+def front_kernel(
     grid_shape,
     own_ref,
     mid_ref,
@@ -37,19 +40,37 @@
     mid_parent_ref,
     mid_weight_ref,
     coarse_ref,
-    win_ref,
+    coarse_in_hbm,
     bias_ref,
-    wout_ref,
+    coarse_out_hbm,
     bias_two_ref,
     gain_ref,
-    window_ref,
+    edge_in_hbm,
+    edge_bias_ref,
+    edges_hbm,
+    tgt_ref,
+    tb_ref,
+    table_hbm,
+    pre_hbm,
     everyone_ref,
     result_ref,
     middle_ref,
+    table_ref,
+    pre_ref,
+    window_ref,
+    edges_ref,
+    target_table,
+    edge_w,
+    win_ref,
+    wout_ref,
     partial,
     arrived_x,
     summed_x,
     arrived_y,
+    local_sem,
+    chunk_sem,
+    pre_sem,
+    table_sem,
     side_send,
     side_recv,
     edge_send,
@@ -68,6 +89,10 @@
     count_x, count_y = grid_shape
     rows_x, rows_y, blk, width = own_ref.shape
     mids = mid_ref.shape[0]
+    lanes = table_ref.shape[-1]
+    parts = width // lanes
+    rows = PAIR * blk
+    chunks = edges_ref.shape[0] // rows
     at_x, at_y = lax.axis_index("gx"), lax.axis_index("gy")
     peers_x = [lax.rem(at_x + offset, count_x) for offset in range(1, count_x)]
     peers_y = [lax.rem(at_y + offset, count_y) for offset in range(1, count_y)]
@@ -78,7 +103,30 @@
         pl.semaphore_signal(barrier, inc=1, device_id=(x, at_y), device_id_type=mesh_ids)
     for y in peers_y:
         pl.semaphore_signal(barrier, inc=1, device_id=(at_x, y), device_id_type=mesh_ids)
-    pl.semaphore_wait(barrier, count_x + count_y - 2)
+
+    loads = [
+        pltpu.make_async_copy(edge_in_hbm, edge_w, local_sem.at[0]),
+        pltpu.make_async_copy(coarse_in_hbm, win_ref, local_sem.at[1]),
+        pltpu.make_async_copy(coarse_out_hbm, wout_ref, local_sem.at[2]),
+    ]
+
+    def chunk_load(i):
+        here = pl.ds(pl.multiple_of(i * rows, rows), rows)
+        return pltpu.make_async_copy(edges_hbm.at[here], edges_ref.at[here], chunk_sem.at[i])
+
+    def pre_store(i):
+        here = pl.ds(pl.multiple_of(i * rows, rows), rows)
+        return pltpu.make_async_copy(pre_ref.at[here], pre_hbm.at[here], pre_sem.at[i])
+
+    def table_store(a, b):
+        number = a * (rows_y + 2) + b
+        here = pl.ds(number * blk * parts, blk * parts)
+        return pltpu.make_async_copy(table_ref.at[here], table_hbm.at[here], table_sem.at[number])
+
+    for load in loads:
+        load.start()
+    for i in range(chunks):
+        chunk_load(i).start()
 
     def remote(src, dst, send, recv, x, y):
         return pltpu.make_async_remote_copy(
@@ -157,8 +205,26 @@
         here = everyone_ref.at[slot]
         return remote(here, here, gx_send.at[x], gx_recv.at[slot], x, at_y)
 
-    start_sides(0)
-    start_sides(1)
+    def fill_table(a, b, block):
+        made = jnp.dot(block, edge_w[1], preferred_element_type=f32) + edge_bias_ref[...] * 0.5
+        for c in range(parts):
+            at = pl.ds((a * (rows_y + 2) + b) * blk * parts + c, blk, stride=parts)
+            table_ref[at, :] = made[:, c * lanes : (c + 1) * lanes]
+        table_store(a, b).start()
+
+    def pre_chunks(first, last):
+        @pl.loop(first, last)
+        def _(i):
+            chunk_load(i).wait()
+            here = pl.ds(pl.multiple_of(i * rows, rows), rows)
+            value = jnp.dot(edges_ref[here, :], edge_w[0], preferred_element_type=f32)
+            from_target = []
+            for k in range(PAIR):
+                target = tgt_ref[pl.ds(i * PAIR + k, 1), :]
+                pick = (lax.broadcasted_iota(jnp.int32, (blk, blk), 0) == target).astype(f32).astype(bf16)
+                from_target.append(first_dims(pick, target_table[tb_ref[i * PAIR + k]]))
+            pre_ref[here, :] = value + jnp.concatenate(from_target, axis=0)
+            pre_store(i).start()
 
     own = own_ref[...].reshape(rows_x * rows_y * blk, width)
     ids = lax.broadcasted_iota(jnp.int32, (mids, own.shape[0]), 0)
@@ -169,9 +235,12 @@
     high, low = split_two(jnp.where(ids == mid_parent_ref[...], mid_weight_ref[...], 0.0))
     sums = jnp.dot(high, middle, preferred_element_type=f32)
     sums = sums + jnp.dot(low, middle, preferred_element_type=f32)
-    partial[...] = sums.reshape(partial.shape)
+    partial[...] = sums.astype(bf16).reshape(partial.shape)
     middle_ref[...] = middle
 
+    pl.semaphore_wait(barrier, count_x + count_y - 2)
+    start_sides(0)
+    start_sides(1)
     for x in peers_x:
         sum_x_copy(x, at_x, x).start()
     for way in range(2):
@@ -180,14 +249,34 @@
         def _():
             edge_copy(way, at_x + ways[way]).start()
 
-    total = partial[at_x]
+    if len(pieces) > 2:
+        start_sides(2)
+
+    loads[0].wait()
+    edge_w[...] = edge_w[...] * 0.5
+    for a in range(rows_x):
+        for b in range(rows_y):
+            block = own_ref[a, b]
+            fill_table(a + 1, b + 1, block)
+            made = jnp.dot(block, edge_w[2], preferred_element_type=f32)
+            target_table[a * rows_y + b] = made.astype(bf16)
+
+    cuts = [chunks * n // 8 for n in (0, 2, 4, 6, 8)]
+    pre_chunks(cuts[0], cuts[1])
+
+    total = partial[at_x].astype(f32)
     for x in peers_x:
         sum_x_copy(x, x, x).wait_recv()
-        total = total + arrived_x[x]
+        total = total + arrived_x[x].astype(f32)
     summed_x[...] = total
+    for y in peers_y:
+        sum_y_copy(y, at_y, y).start()
+
+    pre_chunks(cuts[1], cuts[2])
 
     for side in range(2):
         from_y = at_y - ways[side]
+        column = 0 if ways[side] == 1 else rows_y + 1
 
         @pl.when(has_y(from_y))
         def _():
@@ -199,15 +288,13 @@
                 def _():
                     corner_copy(way, side, at_x + ways[way]).start()
 
-    for y in peers_y:
-        sum_y_copy(y, at_y, y).start()
-    if len(pieces) > 2:
-        start_sides(2)
     restricted = summed_x[at_y]
     for y in peers_y:
         sum_y_copy(y, y, y).wait_recv()
         restricted = restricted + arrived_y[y]
 
+    loads[1].wait()
+    loads[2].wait()
     coarse = coarse_ref[...]
     pre = jnp.dot(coarse, win_ref[0], preferred_element_type=f32)
     pre = pre + jnp.dot(restricted.astype(bf16), win_ref[1], preferred_element_type=f32)
@@ -217,20 +304,53 @@
     result = (coarse.astype(f32) + layer_norm(output, gain_ref[...])).astype(bf16)
     everyone_ref[at_x, at_y] = result
     result_ref[...] = result
+    for y in peers_y:
+        full_y_copy(at_y, y).start()
+
+    pre_chunks(cuts[2], cuts[3])
 
     for way in range(2):
+        row = 0 if ways[way] == 1 else rows_x + 1
 
         @pl.when(has_x(at_x - ways[way]))
         def _():
             edge_copy(way, at_x - ways[way]).wait_recv()
-
-    for y in peers_y:
-        full_y_copy(at_y, y).start()
+            for b in range(rows_y):
+                fill_table(row, b + 1, window_ref[row, b + 1])
+
     for y in peers_y:
         full_y_copy(y, y).wait_recv()
     for x in peers_x:
         full_x_copy(at_x, x).start()
 
+    pre_chunks(cuts[3], cuts[4])
+
+    for side in range(2):
+        column = 0 if ways[side] == 1 else rows_y + 1
+
+        @pl.when(has_y(at_y - ways[side]))
+        def _():
+            for piece in (1, rows_x):
+                fill_table(piece, column, window_ref[piece, column])
+
+        for way in range(2):
+            row = 0 if ways[way] == 1 else rows_x + 1
+
+            @pl.when(has_y(at_y - ways[side]) & has_x(at_x - ways[way]))
+            def _():
+                corner_copy(way, side, at_x - ways[way]).wait_recv()
+                fill_table(row, column, window_ref[row, column])
+
+    if len(pieces) > 2:
+        for side in range(2):
+            column = 0 if ways[side] == 1 else rows_y + 1
+
+            @pl.when(has_y(at_y - ways[side]))
+            def _():
+                side_copy(side, 2, at_y - ways[side]).wait_recv()
+                for a in range(2, rows_x):
+                    fill_table(a, column, window_ref[a, column])
+
     for way in range(2):
 
         @pl.when(has_x(at_x + ways[way]))
@@ -242,21 +362,24 @@
             for piece in range(len(pieces)):
                 side_copy(way, piece, at_y + ways[way]).wait_send()
 
-        if len(pieces) > 2:
-
-            @pl.when(has_y(at_y - ways[way]))
-            def _():
-                side_copy(way, 2, at_y - ways[way]).wait_recv()
-
         for side in range(2):
 
             @pl.when(has_y(at_y - ways[side]) & has_x(at_x + ways[way]))
             def _():
                 corner_copy(way, side, at_x + ways[way]).wait_send()
 
-            @pl.when(has_y(at_y - ways[side]) & has_x(at_x - ways[way]))
+    for a in range(rows_x + 2):
+        for b in range(rows_y + 2):
+            here = (True if a else has_x(at_x - 1)) & (True if a <= rows_x else has_x(at_x + 1))
+            here = here & (True if b else has_y(at_y - 1)) & (True if b <= rows_y else has_y(at_y + 1))
+
+            @pl.when(here)
             def _():
-                corner_copy(way, side, at_x - ways[way]).wait_recv()
+                table_store(a, b).wait()
+
+    @pl.loop(0, chunks)
+    def _(i):
+        pre_store(i).wait()
 
     for x in peers_x:
         sum_x_copy(x, at_x, x).wait_send()
@@ -267,29 +390,46 @@
         full_y_copy(at_y, y).wait_send()
 
 
-def exchange(own, middle, parents, weights, mid_parents, mid_weights, coarse, params):
+def run_front(own, middle, parents, weights, mid_parents, mid_weights, coarse, params, edges, edge_in, edge_bias, targets, blocks):
     rows_x, rows_y, blk, width = own.shape
     count_x, count_y = lax.axis_size("gx"), lax.axis_size("gy")
     coarse_own = coarse.shape[0]
     coarse_in, bias, coarse_out, bias_two, gain = params
     row = lambda array: array.reshape(1, -1)
     vmem = pl.BlockSpec(memory_space=pltpu.VMEM)
+    away = pl.BlockSpec(memory_space=pl.ANY)
+    smem = pl.BlockSpec(memory_space=pltpu.SMEM)
     dma = pltpu.SemaphoreType.DMA
+    lanes = 128
+    edge_rows = edges.shape[0]
     return pl.pallas_call(
-        functools.partial(exchange_kernel, (count_x, count_y)),
-        in_specs=[vmem] * 12,
-        out_specs=[vmem] * 4,
+        functools.partial(front_kernel, (count_x, count_y)),
+        in_specs=[vmem] * 7 + [away, vmem, away, vmem, vmem, away, vmem, away, vmem, smem],
+        out_specs=[away] * 2 + [vmem] * 3,
         out_shape=[
-            jax.ShapeDtypeStruct((rows_x + 2, rows_y + 2, blk, width), bf16),
+            TABLE((rows_x + 2) * (rows_y + 2) * blk * (width // lanes), lanes),
+            TABLE(edge_rows, width),
             jax.ShapeDtypeStruct((count_x, count_y, coarse_own, width), bf16),
             jax.ShapeDtypeStruct((coarse_own, width), bf16),
             jax.ShapeDtypeStruct(middle.shape, bf16),
         ],
         scratch_shapes=[
-            pltpu.VMEM((count_x, count_y, coarse_own, width), f32),
-            pltpu.VMEM((count_x, count_y, coarse_own, width), f32),
+            pltpu.VMEM(((rows_x + 2) * (rows_y + 2) * blk * (width // lanes), lanes), f32),
+            pltpu.VMEM(edges.shape, f32),
+            pltpu.VMEM((rows_x + 2, rows_y + 2, blk, width), bf16),
+            pltpu.VMEM(edges.shape, bf16),
+            pltpu.VMEM((rows_x * rows_y, blk, width), bf16),
+            pltpu.VMEM(edge_in.shape, bf16),
+            pltpu.VMEM(coarse_in.shape, bf16),
+            pltpu.VMEM(coarse_out.shape, bf16),
+            pltpu.VMEM((count_x, count_y, coarse_own, width), bf16),
+            pltpu.VMEM((count_x, count_y, coarse_own, width), bf16),
             pltpu.VMEM((count_y, coarse_own, width), f32),
             pltpu.VMEM((count_y, coarse_own, width), f32),
+            dma((3,)),
+            dma((edge_rows // (PAIR * blk),)),
+            dma((edge_rows // (PAIR * blk),)),
+            dma(((rows_x + 2) * (rows_y + 2),)),
             dma((2, 3)),
             dma((2, 3)),
             dma((2,)),
@@ -305,8 +445,10 @@
             dma((count_y,)),
             dma((count_y,)),
         ],
-        compiler_params=pltpu.CompilerParams(collective_id=0, has_side_effects=True),
-        name="exchange",
+        compiler_params=pltpu.CompilerParams(
+            collective_id=0, has_side_effects=True, vmem_limit_bytes=FRONT_VMEM
+        ),
+        name="front",
     )(
         own,
         middle,
@@ -320,6 +462,11 @@
         coarse_out,
         row(bias_two),
         row(gain),
+        edge_in,
+        row(edge_bias),
+        edges,
+        targets,
+        blocks,
     )
 
 
@@ -328,20 +475,15 @@
     src_ref,
     tb_ref,
     live_ref,
-    own_ref,
-    window_ref,
+    table,
+    pre_ref,
     edge_ref,
     tgt_ref,
-    win_ref,
-    bias_ref,
     wout_ref,
     bias_two_ref,
     gain_ref,
     out_ref,
     agg_ref,
-    table,
-    target_table,
-    first_w,
     buf_a,
     buf_b,
     total,
@@ -364,21 +506,11 @@
     def compute(first_block, local, buf):
         rows = PAIR * blk
         start = local * blk
-        edges = edge_ref[pl.ds(start, rows), :]
-        pre = jnp.dot(edges, first_w[...], preferred_element_type=f32)
         found = buf[...].reshape(rows // 8, parts, 8, lanes)
         found = jnp.concatenate(
             [found[:, c].reshape(rows, lanes) for c in range(parts)], axis=1
         )
-        picks = []
-        from_target = []
-        for k in range(PAIR):
-            target = tgt_ref[pl.ds(local + k, 1), :]
-            pick = (lax.broadcasted_iota(jnp.int32, (blk, blk), 0) == target).astype(f32).astype(bf16)
-            picks.append(pick)
-            here = pl.multiple_of(tb_ref[first_block + k] * blk, blk)
-            from_target.append(first_dims(pick, target_table[pl.ds(here, blk), :]))
-        half = pre + jnp.concatenate(from_target, axis=0) + found
+        half = pre_ref[pl.ds(start, rows), :] + found
         hidden = (half + half * jnp.tanh(half)).astype(bf16)
         output = jnp.dot(hidden, wout_ref[...], preferred_element_type=f32) + bias_two_ref[...]
         centred = output - jnp.mean(output, axis=-1, keepdims=True)
@@ -388,28 +520,16 @@
             alive = (first_block + k < live).astype(f32)
             part = slice(k * blk, (k + 1) * blk)
             message = (normed[part] * (gain_ref[...] * alive)).astype(bf16)
-            out_ref[pl.ds(start + k * blk, blk), :] = edges[part] + message
+            here = pl.ds(start + k * blk, blk)
+            out_ref[here, :] = edge_ref[here, :] + message
+            target = tgt_ref[pl.ds(local + k, 1), :]
+            pick = (lax.broadcasted_iota(jnp.int32, (blk, blk), 0) == target).astype(f32).astype(bf16)
             here = pl.multiple_of(tb_ref[first_block + k] * blk, blk)
-            total[pl.ds(here, blk), :] += jnp.dot(picks[k], message, preferred_element_type=f32)
+            total[pl.ds(here, blk), :] += jnp.dot(pick, message, preferred_element_type=f32)
 
     @pl.when(step == 0)
     def _():
         total[...] = jnp.zeros_like(total)
-        first_w[...] = win_ref[0] * 0.5
-        for a in range(rows_x + 2):
-            for b in range(rows_y + 2):
-                number = a * (rows_y + 2) + b
-                mine = 1 <= a <= rows_x and 1 <= b <= rows_y
-                rows = own_ref[a - 1, b - 1] if mine else window_ref[a, b]
-                made = jnp.dot(rows, win_ref[1], preferred_element_type=f32)
-                made = (made + bias_ref[...]) * 0.5
-                for c in range(parts):
-                    at = pl.ds(number * blk * parts + c, blk, stride=parts)
-                    table[at, :] = made[:, c * lanes : (c + 1) * lanes]
-                if mine:
-                    made = jnp.dot(rows, win_ref[2], preferred_element_type=f32) * 0.5
-                    at = ((a - 1) * rows_y + b - 1) * blk
-                    target_table[pl.ds(at, blk), :] = made.astype(bf16)
         gather(0, buf_a)
 
     @pl.when(step * per_step < live)
@@ -430,48 +550,44 @@
         agg_ref[...] = total[...].astype(bf16)
 
 
-def run_edges(own, window, edges, sources, block_target, node_target, live, params):
-    pieces = [own, window]
-    rows_x, rows_y, blk, width = own.shape
-    edge_in, bias, edge_out, bias_two, gain = params
-    edge_blocks = edges.shape[0]
+def run_edges(shape, table, pre, edges, sources, block_target, targets, live, params):
+    rows_x, rows_y, blk, width = shape
+    edge_out, bias_two, gain = params
+    edge_blocks = edges.shape[0] // blk
     per_step = 2 * PAIR
     lanes = 128
     whole = lambda array: pl.BlockSpec(array.shape, lambda i, *_: (0,) * array.ndim)
-    flat = edges.reshape(edge_blocks * blk, width)
-    targets = node_target.reshape(edge_blocks // per_step, per_step, blk)
-    small = [bias.reshape(1, width), edge_out, bias_two.reshape(1, width), gain.reshape(1, width)]
+    targets = targets.reshape(edge_blocks // per_step, per_step, blk)
+    small = [edge_out, bias_two.reshape(1, width), gain.reshape(1, width)]
     own_count = rows_x * rows_y * blk
     row_spec = pl.BlockSpec((per_step * blk, width), lambda i, *_: (i, 0))
     return pl.pallas_call(
-        functools.partial(edge_kernel, own.shape),
+        functools.partial(edge_kernel, shape),
         grid_spec=pltpu.PrefetchScalarGridSpec(
             num_scalar_prefetch=3,
             grid=(edge_blocks // per_step,),
-            in_specs=[whole(p) for p in pieces]
-            + [row_spec, pl.BlockSpec((None, per_step, blk), lambda i, *_: (i, 0, 0)), whole(edge_in)]
+            in_specs=[pl.BlockSpec(memory_space=pltpu.VMEM), row_spec, row_spec]
+            + [pl.BlockSpec((None, per_step, blk), lambda i, *_: (i, 0, 0))]
             + [whole(s) for s in small],
             out_specs=[row_spec, pl.BlockSpec((own_count, width), lambda i, *_: (0, 0))],
             scratch_shapes=[
-                pltpu.VMEM(((rows_x + 2) * (rows_y + 2) * blk * (width // lanes), lanes), f32),
-                pltpu.VMEM((own_count, width), bf16),
-                pltpu.VMEM((width, width), bf16),
                 pltpu.VMEM((PAIR * blk * width // lanes, lanes), f32),
                 pltpu.VMEM((PAIR * blk * width // lanes, lanes), f32),
                 pltpu.VMEM((own_count, width), f32),
             ],
         ),
         out_shape=[
-            jax.ShapeDtypeStruct(flat.shape, bf16),
+            jax.ShapeDtypeStruct(edges.shape, bf16),
             jax.ShapeDtypeStruct((own_count, width), bf16),
         ],
+        compiler_params=pltpu.CompilerParams(vmem_limit_bytes=EDGE_VMEM),
         cost_estimate=pl.CostEstimate(
-            flops=8 * flat.shape[0] * width * width,
-            bytes_accessed=4 * flat.size,
-            transcendentals=flat.size,
+            flops=4 * edges.shape[0] * width * width,
+            bytes_accessed=8 * edges.size,
+            transcendentals=edges.size,
         ),
         name="edge_layer",
-    )(sources.reshape(-1), block_target, live.reshape(1), *pieces, flat, targets, edge_in, *small)
+    )(sources.reshape(-1), block_target, live.reshape(1), table, pre, edges, targets, *small)
 
 
 def node_kernel(
@@ -488,8 +604,10 @@
     wout_ref,
     bias_two_ref,
     gain_ref,
+    own_coarse_ref,
     out_ref,
     mid_out_ref,
+    own_coarse_out_ref,
     doubled,
 ):
     mids = mid_ref.shape[0]
@@ -503,6 +621,7 @@
         value = mid_ref[...].astype(f32) + first_dims(high, coarse) + first_dims(low, coarse)
         value = value.astype(bf16)
         mid_out_ref[...] = value
+        own_coarse_out_ref[...] = own_coarse_ref[...]
         doubled[pl.ds(0, mids), :] = value
         doubled[pl.ds(mids, mids), :] = value
 
@@ -518,7 +637,7 @@
     out_ref[...] = (fine + from_middle).astype(bf16)
 
 
-def run_nodes(own, agg, parents, weights, middle, mid_parents, mid_weights, coarse, params):
+def run_nodes(own, agg, parents, weights, middle, mid_parents, mid_weights, coarse, own_coarse, params):
     count, width = own.shape
     node_in, bias, node_out, bias_two, gain = params
     tile = 256 if count % 256 == 0 else 128
@@ -527,13 +646,17 @@
     across = pl.BlockSpec((1, tile), lambda i: (0, i))
     row = lambda array: array.reshape(1, -1)
     fixed = [middle, row(mid_parents), row(mid_weights), coarse]
-    fixed += [node_in, row(bias), node_out, row(bias_two), row(gain)]
+    fixed += [node_in, row(bias), node_out, row(bias_two), row(gain), own_coarse]
     return pl.pallas_call(
         node_kernel,
         grid=(count // tile,),
         in_specs=[rows, rows, across, across] + [whole(f) for f in fixed],
-        out_specs=[rows, whole(middle)],
-        out_shape=[jax.ShapeDtypeStruct(own.shape, bf16), jax.ShapeDtypeStruct(middle.shape, bf16)],
+        out_specs=[rows, whole(middle), whole(own_coarse)],
+        out_shape=[
+            jax.ShapeDtypeStruct(own.shape, bf16),
+            jax.ShapeDtypeStruct(middle.shape, bf16),
+            jax.ShapeDtypeStruct(own_coarse.shape, bf16),
+        ],
         scratch_shapes=[pltpu.VMEM((2 * middle.shape[0], width), bf16)],
         cost_estimate=pl.CostEstimate(
             flops=8 * count * width * width, bytes_accessed=8 * own.size, transcendentals=own.size
@@ -574,7 +697,6 @@
     rows_x, rows_y, block_size, latent = fine_nodes.shape
     own_count = rows_x * rows_y * block_size
     own_rows = fine_nodes.reshape(own_count, latent)
-    edge_params = (edge_in, edge_bias, edge_out, edge_bias_two, edge_gain)
     node_params = (node_in, node_bias, node_out, node_bias_two, node_gain)
     parents_local = fine_parent.reshape(own_count)
     weights_local = fine_weight.reshape(own_count)
@@ -583,7 +705,10 @@
     mid_weights = middle_weight[0, 0]
     coarse_own = coarse_nodes.shape[0]
     devices = lax.axis_size(("gx", "gy"))
-    window, everyone, coarse_result, middle_mid = exchange(
+    edge_blocks = edge_states.shape[2]
+    edges = edge_states.reshape(edge_blocks * block_size, latent)
+    targets = target_nodes[0, 0]
+    table, pre, everyone, coarse_own_rows, middle_mid = run_front(
         fine_nodes,
         middle_rows,
         parents_local,
@@ -592,19 +717,25 @@
         mid_weights,
         coarse_nodes,
         (coarse_in, coarse_bias, coarse_out, coarse_bias_two, coarse_gain),
+        edges,
+        edge_in,
+        edge_bias,
+        targets,
+        target_blocks[0, 0],
     )
     everyone = everyone.reshape(devices * coarse_own, latent)
     edge_result, aggregate = run_edges(
-        fine_nodes,
-        window,
-        edge_states[0, 0],
+        fine_nodes.shape,
+        table,
+        pre,
+        edges,
         edge_sources[0, 0],
         target_blocks[0, 0],
-        target_nodes[0, 0],
+        targets,
         live_blocks[0, 0],
-        edge_params,
+        (edge_out, edge_bias_two, edge_gain),
     )
-    fine_result, middle_result = run_nodes(
+    fine_result, middle_result, coarse_result = run_nodes(
         own_rows,
         aggregate,
         parents_local,
@@ -613,6 +744,7 @@
         mid_parents,
         mid_weights,
         everyone,
+        coarse_own_rows,
         node_params,
     )
     return (

time: 74.9 us -> 66.8 us (0.89)
  the two profiles are of different devices: /device:TPU:1 before, /device:TPU:8 now
where the time goes in v1:
time: 66.8 us; the launch traced here: 65.7 us
  Pallas kernels  64.4 us (96%)
  between operations  1.29 us (2%)
    pallas_call x1, Pallas kernels, run_front(): pl.pallas_call(functools.partial(front_kernel, (count_x, count_y)), in_sp...  30 us
    pallas_call x1, Pallas kernels, run_edges(): pl.pallas_call(functools.partial(edge_kernel, shape), grid_spec=pltpu.Pre...  27.6 us
    pallas_call x1, Pallas kernels, run_nodes(): pl.pallas_call(node_kernel, grid=(count // tile,), in_specs=[rows, rows,...  6.85 us

profile of v1, /device:TPU:8, one launch (start us, length us, event | category | flops | bytes accessed | tf_op | source)
XLA Modules:
  0.0 65.7 jit_solution(16912214942722316660)
XLA Ops:
  1.3 30.0 %front.1 = (f32[12288,128]{1,0:T(8,128)}, f32[8192,512]{1,0:T(8,128)}, bf16[8,4,8,512]{3,2,1,0:T(8,128)(2,1)}, bf16[8,512]{1,0:T(8,128)(2,1)}, bf16[128,512]{1,0:T(8,128)(2,1)}) custom-call(bf16[4,2,128,512]{3,2,1,0:T(8,128)(2,1)} %own_ref.1, bf16[128,512]{1,0:T(8,128)(2,1)} %bitcast.29, s32[1,1024]{1,0:T(1,128)} %bitcast.33, f32[1,1024]{1,0:T(1,128)} %bitcast.35, ...), custom_call_target="tpu_custom_call" | custom-call | tf_op jit(solution)/shard_map/front/pallas_call | solution.py:405
  31.3 27.6 %edge_layer.1 = (bf16[8192,512]{1,0:T(8,128)(2,1)}, bf16[1024,512]{1,0:T(8,128)(2,1)}) custom-call(s32[8192]{0:T(1024)} %bitcast.32, s32[64]{0:T(128)} %bitcast.44, s32[1]{0:T(128)} %bitcast.25.live_ref, f32[12288,128]{1,0:T(8,128)} %get-tuple-element.14.table, f32[8192,512]{1,0:T(8,128)} %get-tuple-element.15.pre_ref, bf16[8192,512]{1,0:T(8,128)(2,1)} %bitcast.27, ...), custom_call_target="tpu_custom_call" | custom-call | flops 8589934592 | bytes 33554432 | tf_op jit(solution)/shard_map/edge_layer/pallas_call | solution.py:564
  58.9 6.9 %node_layer.1 = (bf16[1024,512]{1,0:T(8,128)(2,1)}, bf16[128,512]{1,0:T(8,128)(2,1)}, bf16[8,512]{1,0:T(8,128)(2,1)}) custom-call(bf16[1024,512]{1,0:T(8,128)(2,1)} %bitcast.28, bf16[1024,512]{1,0:T(8,128)(2,1)} %get-tuple-element.16.agg_ref, s32[1,1024]{1,0:T(1,128)} %bitcast.34, f32[1,1024]{1,0:T(1,128)} %bitcast.36, ...), custom_call_target="tpu_custom_call" | custom-call | flops 2147483648 | bytes 4194304 | tf_op jit(solution)/shard_map/node_layer/pallas_call | solution.py:650
